TPU v7x, 1024 devices: a whole 8x8x8 slice. The times are simulated.
1024 devices in a mesh: gz: 64 (over x_lo, y, core), xy: 16 (over x_hi, z).
Axes of the slice: x: 8 (x_hi: 2, x_lo: 4; x = x_hi * 4 + x_lo), y: 8, z: 8, core: 2. Of those that a mesh axis runs over, the one named last changes fastest.
Arguments:
- flux_xface: bfloat16 [64, 2048, 2048], P(None, 'gz', 'xy'), may hold values from -6 to 6
- flux_yspec: bfloat16 [64, 2048, 2048], P(None, 'gz', 'xy'), may hold values from -6 to 6
- flux_zface: bfloat16 [64, 2048, 2048], P(None, 'gz', 'xy'), may hold values from -6 to 6
- frequency_y: int32 [64], replicated, may hold values from 0 to 2047
Outputs:
- potential: float32 [64, 2048, 2, 1024], P('gz', 'xy')
All inputs are finite; a program needn't handle non-finite values.
Results may differ from a plain program's by a relative error of at most 0.0003.
Values may be sent and summed in bfloat16 or wider, within the bound.
A program may use at most 32 MiB of HBM per device.

v0:
```python
import math

import jax
import jax.numpy as jnp
from jax import lax
from jax.sharding import PartitionSpec as P

NX = 2048
NY = 2048
NZ = 2048


SCREEN_WEIGHT = 0.5


def shifted(block, axis, distance):
    devices = range(lax.axis_size(axis))
    route = [(i - distance, i) for i in devices if i - distance in devices]
    return lax.ppermute(block, axis, route)


def cosine_table(length, parity):
    halved = length // 2
    row_index = lax.broadcasted_iota(jnp.int32, (halved, halved), 0)
    col_index = lax.broadcasted_iota(jnp.int32, (halved, halved), 1)
    frequency = 2 * row_index + parity
    phase = frequency * (2 * col_index + 1) % (4 * length)
    scaling = jnp.where(frequency == 0, math.sqrt(1.0 / length), math.sqrt(2.0 / length)).astype(
        jnp.float32
    )
    return scaling * jnp.cos(phase.astype(jnp.float32) * (math.pi / (2 * length)))


def fold_middle(source):
    length = source.shape[1]
    halved = length // 2
    upper_half = source[:, :halved]
    lower_half = lax.rev(source[:, halved:], (1,))
    even_part = jnp.einsum(
        "kq,fql->fkl",
        cosine_table(length, 0),
        upper_half + lower_half,
        precision=lax.Precision.HIGHEST,
    )
    odd_part = jnp.einsum(
        "kq,fql->fkl",
        cosine_table(length, 1),
        upper_half - lower_half,
        precision=lax.Precision.HIGHEST,
    )
    return jnp.stack([even_part, odd_part], axis=2).reshape(source.shape)


def fold_last(source):
    length = source.shape[2]
    halved = length // 2
    upper_half = source[:, :, :halved]
    lower_half = lax.rev(source[:, :, halved:], (2,))
    even_part = jnp.einsum(
        "yzn,mn->yzm",
        upper_half + lower_half,
        cosine_table(length, 0),
        precision=lax.Precision.HIGHEST,
    )
    odd_part = jnp.einsum(
        "yzn,mn->yzm",
        upper_half - lower_half,
        cosine_table(length, 1),
        precision=lax.Precision.HIGHEST,
    )
    return jnp.stack([even_part, odd_part], axis=2)


def eigenvalue(index, length):
    sine = jnp.sin(index.astype(jnp.float32) * (math.pi / (2 * length)))
    return 4.0 * sine * sine


def shards(flux_xface, flux_yspec, flux_zface, frequency_y):
    x_rank = lax.axis_index("xy")
    x_count = lax.axis_size("xy")
    z_rank = lax.axis_index("gz")
    z_count = lax.axis_size("gz")
    planes = flux_xface.shape[1]
    x_width = flux_xface.shape[2]
    x_position = lax.broadcasted_iota(jnp.int32, flux_xface.shape, 2)
    x_keep = jnp.logical_not((x_rank == x_count - 1) & (x_position == x_width - 1))
    masked_x = jnp.where(x_keep, flux_xface, jnp.zeros_like(flux_xface))
    x_edge = shifted(masked_x[:, :, x_width - 1 :], "xy", 1)
    x_before = jnp.concatenate([x_edge, masked_x[:, :, : x_width - 1]], axis=2)
    weight_y = 2.0 * jnp.sin(frequency_y.astype(jnp.float32) * (math.pi / (2 * NY)))
    partial_value = (
        masked_x.astype(jnp.float32)
        - x_before.astype(jnp.float32)
        + weight_y[:, None, None] * flux_yspec.astype(jnp.float32)
    )
    z_position = lax.broadcasted_iota(jnp.int32, flux_zface.shape, 1)
    z_keep = jnp.logical_not((z_rank == z_count - 1) & (z_position == planes - 1))
    masked_z = jnp.where(z_keep, flux_zface, jnp.zeros_like(flux_zface))
    z_edge = shifted(masked_z[:, planes - 1 :, :], "gz", 1)
    z_before = jnp.concatenate([z_edge, masked_z[:, : planes - 1]], axis=1)
    slab = partial_value + masked_z.astype(jnp.float32) - z_before.astype(jnp.float32)
    totals = lax.all_to_all(slab, "gz", split_axis=0, concat_axis=1, tiled=True)
    spectrum_z = fold_middle(totals)
    x_lines = lax.all_to_all(spectrum_z, "xy", split_axis=1, concat_axis=2, tiled=True)
    spectrum = fold_last(x_lines)
    row_count = spectrum.shape[0]
    kz_count = spectrum.shape[1]
    halved = spectrum.shape[3]
    local_freq = lax.dynamic_slice_in_dim(frequency_y, z_rank * row_count, row_count)
    weight_local = 2.0 * jnp.sin(local_freq.astype(jnp.float32) * (math.pi / (2 * NY)))
    kz_index = x_rank * kz_count + lax.broadcasted_iota(jnp.int32, (kz_count,), 0)
    kx_index = 2 * lax.broadcasted_iota(jnp.int32, (2, halved), 1) + lax.broadcasted_iota(
        jnp.int32, (2, halved), 0
    )
    denominator = (
        (weight_local * weight_local)[:, None, None, None]
        + eigenvalue(kz_index, NZ)[None, :, None, None]
        + eigenvalue(kx_index, NX)[None, None, :, :]
        + SCREEN_WEIGHT
    )
    return -spectrum / denominator


def solution(mesh):
    return jax.shard_map(
        shards,
        mesh=mesh,
        in_specs=(P(None, "gz", "xy"), P(None, "gz", "xy"), P(None, "gz", "xy"), P()),
        out_specs=P("gz", "xy", None, None),
        check_vma=False,
    )
```

profile of v0, /device:TPU:18, one launch (start us, length us, event | category | flops | bytes accessed | tf_op | source)
XLA Modules:
  0.0 212.3 jit_solution(5400231000630875534)
XLA Ops:
  0.0 0.0 copy-start
  0.0 1.2 broadcast_select_fusion
  1.3 1.9 collective-permute-start.1
  3.2 0.0 copy-done
  3.2 0.0 copy-start.3
  3.2 0.0 copy-start.1
  3.2 0.0 copy-start.2
  3.3 0.2 slice.32
  3.5 5.3 %collective-permute-start = (bf16[64,32,1]{2,1,0:T(8,128)(2,1)S(1)}, bf16[64,32,1]{2,1,0:T(8,128)(2,1)S(1)}, u32[]{:S(2)}, u32[]{:S(2)}) collective-permute-start(bf16[64,32,1]{2,1,0:T(8,128)(2,1)S(1)} %slice.32), channel_id=1, source_target_pairs={{0,1},{1,2},{2,3},{3,4},{4,5},{5,6},{6,7},{7,8},{8,9},{9,10},{10,1... | collective-permute-start | bytes 12296 | tf_op jit(solution)/shard_map/ppermute | solution.py:19
  8.9 0.0 copy-done.3
  8.9 11.4 %collective-permute-done = bf16[64,32,1]{2,1,0:T(8,128)(2,1)S(1)} collective-permute-done((bf16[64,32,1]{2,1,0:T(8,128)(2,1)S(1)}, bf16[64,32,1]{2,1,0:T(8,128)(2,1)S(1)}, u32[]{:S(2)}, u32[]{:S(2)}) %collective-permute-start) | collective-permute-done | bytes 4128 | tf_op jit(solution)/shard_map/ppermute | solution.py:19
  20.3 0.0 collective-permute-done.1
  20.3 0.0 copy-done.1
  20.3 0.0 copy-done.2
  20.3 1.8 convert_subtract_fusion
  22.1 12.0 %all-to-all-start = ((f32[64,32,128]{2,1,0:T(8,128)}), f32[64,32,128]{2,1,0:T(8,128)S(1)}, u32[]{:S(2)}, u32[]{:S(2)}) async-start(f32[64,32,128]{2,1,0:T(8,128)} %convert_subtract_fusion), calls=%async_computation | async-start | bytes 2097152 | tf_op jit(solution)/shard_map/all_to_all | solution.py:103
  34.2 27.5 %all-to-all-done = f32[64,32,128]{2,1,0:T(8,128)S(1)} async-done(((f32[64,32,128]{2,1,0:T(8,128)}), f32[64,32,128]{2,1,0:T(8,128)S(1)}, u32[]{:S(2)}, u32[]{:S(2)}) %all-to-all-start) | async-done | bytes 1048608 | tf_op jit(solution)/shard_map/all_to_all | solution.py:103
  61.7 0.7 rev.6
  62.4 20.2 %fusion.24 = f32[1,1024,1,128]{1,3,2,0:T(8,128)S(1)} fusion(s32[1024]{0:T(1024)S(1)} %get-tuple-element.6, f32[1024]{0:T(1024)S(1)} %compare_select_fusion, f32[1,1024,128]{2,1,0:T(8,128)S(1)} %rev.6, f32[1,2048,128]{2,1,0:T(8,128)S(1)} %bitcast.42), kind=kOutput, calls=%fused_computation.26 | convolution fusion | flops 1626472448 | bytes 1585152 | tf_op jit(solution)/shard_map/kq,fql->fkl/dot_general | solution.py:45
  82.7 20.7 %fusion.18 = f32[1,1024,1,128]{1,3,2,0:T(8,128)S(1)} fusion(s32[1024]{0:T(1024)S(1)} %get-tuple-element.6, s32[1024]{0:T(1024)S(1)} %get-tuple-element.5, f32[1024]{0:T(1024)S(1)} %compare_select_fusion.1, f32[1,1024,128]{2,1,0:T(8,128)S(1)} %rev.6, f32[1,2048,128]{2,1,0:T(8,128)S(1)} %bitcast.43), kind=kOutput, calls=%fused_computation.24 | convolution fusion | flops 1626472448 | bytes 1585152 | tf_op jit(solution)/shard_map/kq,fql->fkl/dot_general | solution.py:39
  103.4 0.1 pad_maximum_fusion
  103.5 1.3 copy.12
  104.8 29.8 %all-to-all-start.1 = ((f32[1,2048,128]{2,0,1:T(1,128)}), f32[1,2048,128]{2,0,1:T(1,128)S(1)}, u32[]{:S(2)}, u32[]{:S(2)}) async-start(f32[1,2048,128]{2,0,1:T(1,128)} %bitcast.10), calls=%async_computation.1 | async-start | bytes 2097152 | tf_op jit(solution)/shard_map/all_to_all | solution.py:105
  134.6 0.6 dynamic_slice.3
  136.0 0.1 multiply_multiply_fusion
  136.2 32.4 %all-to-all-done.1 = f32[1,2048,128]{2,0,1:T(1,128)S(1)} async-done(((f32[1,2048,128]{2,0,1:T(1,128)}), f32[1,2048,128]{2,0,1:T(1,128)S(1)}, u32[]{:S(2)}, u32[]{:S(2)}) %all-to-all-start.1) | async-done | bytes 1048608 | tf_op jit(solution)/shard_map/all_to_all | solution.py:105
  168.5 0.3 copy.14
  168.9 0.2 rev.7
  169.1 20.5 %fusion.21 = f32[1,128,1,1024]{3,1,2,0:T(8,128)S(1)} fusion(s32[1024]{0:T(1024)S(1)} %get-tuple-element.6, s32[1024]{0:T(1024)S(1)} %get-tuple-element.5, f32[1024]{0:T(1024)S(1)} %compare_select_fusion.1, f32[1,128,1024]{1,2,0:T(8,128)S(1)} %rev.7, f32[1,128,2048]{1,2,0:T(8,128)S(1)} %bitcast.45), kind=kOutput, calls=%fused_computation.25 | convolution fusion | flops 1626472448 | bytes 1585152 | tf_op jit(solution)/shard_map/yzn,mn->yzm/dot_general | solution.py:59
  189.6 20.4 %fusion.27 = f32[1,128,1,1024]{3,1,2,0:T(8,128)S(1)} fusion(s32[1024]{0:T(1024)S(1)} %get-tuple-element.6, f32[1024]{0:T(1024)S(1)} %compare_select_fusion, f32[1,128,1024]{1,2,0:T(8,128)S(1)} %rev.7, f32[1,128,2048]{1,2,0:T(8,128)S(1)} %bitcast.46), kind=kOutput, calls=%fused_computation.27 | convolution fusion | flops 1626472448 | bytes 1585152 | tf_op jit(solution)/shard_map/yzn,mn->yzm/dot_general | solution.py:65
  210.1 0.2 fusion.30
  210.3 1.8 copy.15
  (11 shorter events, 0.3 us)
Async XLA Ops:
  0.0 3.2 %copy-start = (bf16[64,32,128]{2,1,0:T(8,128)(2,1)S(1)}, bf16[64,32,128]{2,1,0:T(8,128)(2,1)}, u32[]{:S(2)}) copy-start(bf16[64,32,128]{2,1,0:T(8,128)(2,1)} %param.4) | copy-start | bytes 1572868
  1.3 19.1 %collective-permute-start.1 = (bf16[64,1,128]{2,1,0:T(2,128)(2,1)S(1)}, bf16[64,1,128]{2,1,0:T(2,128)(2,1)S(1)}, u32[]{:S(2)}, u32[]{:S(2)}) collective-permute-start(bf16[64,1,128]{2,1,0:T(2,128)(2,1)S(1)} %slice.34), channel_id=1, source_target_pairs={{0,16},{16,32},{32,48},{48,64},{64,80},{80,96},{96,112},{112,128},... | collective-permute-start | bytes 49160 | tf_op jit(solution)/shard_map/ppermute | solution.py:19
  3.2 5.7 %copy-start.3 = (s32[64]{0:T(128)S(1)}, s32[64]{0:T(128)}, u32[]{:S(2)}) copy-start(s32[64]{0:T(128)} %param.7) | copy-start | bytes 772
  3.2 17.1 %copy-start.1 = (bf16[64,32,128]{2,1,0:T(8,128)(2,1)S(1)}, bf16[64,32,128]{2,1,0:T(8,128)(2,1)}, u32[]{:S(2)}) copy-start(bf16[64,32,128]{2,1,0:T(8,128)(2,1)} %param.6) | copy-start | bytes 1572868
  3.2 17.1 %copy-start.2 = (bf16[64,32,128]{2,1,0:T(8,128)(2,1)S(1)}, bf16[64,32,128]{2,1,0:T(8,128)(2,1)}, u32[]{:S(2)}) copy-start(bf16[64,32,128]{2,1,0:T(8,128)(2,1)} %param.5) | copy-start | bytes 1572868
  3.5 16.8 %collective-permute-start = (bf16[64,32,1]{2,1,0:T(8,128)(2,1)S(1)}, bf16[64,32,1]{2,1,0:T(8,128)(2,1)S(1)}, u32[]{:S(2)}, u32[]{:S(2)}) collective-permute-start(bf16[64,32,1]{2,1,0:T(8,128)(2,1)S(1)} %slice.32), channel_id=1, source_target_pairs={{0,1},{1,2},{2,3},{3,4},{4,5},{5,6},{6,7},{7,8},{8,9},{9,10},{10,1... | collective-permute-start | bytes 12296 | tf_op jit(solution)/shard_map/ppermute | solution.py:19
  22.1 39.5 %all-to-all-start = ((f32[64,32,128]{2,1,0:T(8,128)}), f32[64,32,128]{2,1,0:T(8,128)S(1)}, u32[]{:S(2)}, u32[]{:S(2)}) async-start(f32[64,32,128]{2,1,0:T(8,128)} %convert_subtract_fusion), calls=%async_computation | async-start | bytes 2097152 | tf_op jit(solution)/shard_map/all_to_all | solution.py:103
  104.8 63.8 %all-to-all-start.1 = ((f32[1,2048,128]{2,0,1:T(1,128)}), f32[1,2048,128]{2,0,1:T(1,128)S(1)}, u32[]{:S(2)}, u32[]{:S(2)}) async-start(f32[1,2048,128]{2,0,1:T(1,128)} %bitcast.10), calls=%async_computation.1 | async-start | bytes 2097152 | tf_op jit(solution)/shard_map/all_to_all | solution.py:105
where the time goes:
time: 215 us; the launch traced here: 212 us
  matrix products  81.8 us (38%)
  waiting for transfers between devices  71.3 us (33%)
  starting transfers between devices  49.1 us (23%)
  local copies, waits for them, and re-layouts  5.31 us (2%)
  other arithmetic  3.64 us (2%)
    all_to_all x1, waiting for transfers between devices, shards(): lax.all_to_all(spectrum_z, 'xy', split_axis=1, concat_axis=2, tiled=True)  32.4 us
    all_to_all x1, starting transfers between devices, shards(): lax.all_to_all(spectrum_z, 'xy', split_axis=1, concat_axis=2, tiled=True)  29.8 us
    all_to_all x1, waiting for transfers between devices, shards(): totals = lax.all_to_all(slab, 'gz', split_axis=0, concat_axis=1, tiled=True)  27.5 us
    dot_general x1, matrix products, fold_middle(): jnp.einsum('kq,fql->fkl', cosine_table(length, 0), upper_half + lower_hal...  20.7 us
    dot_general x1, matrix products, fold_last(): jnp.einsum('yzn,mn->yzm', upper_half + lower_half, cosine_table(length, 0...  20.5 us
    dot_general x1, matrix products, fold_last(): jnp.einsum('yzn,mn->yzm', upper_half - lower_half, cosine_table(length, 1...  20.4 us
    dot_general x1, matrix products, fold_middle(): jnp.einsum('kq,fql->fkl', cosine_table(length, 1), upper_half - lower_hal...  20.2 us
    all_to_all x1, starting transfers between devices, shards(): totals = lax.all_to_all(slab, 'gz', split_axis=0, concat_axis=1, tiled=True)  12 us
  transfers between devices with their start and end apart: 4, of which 3 were waited for; matrix products, arithmetic and copies ran while one was open for 1% of the time, Pallas kernels for 0%

commit v1 on v0

v1 whole, which is shorter than its diff:
```python
import functools
import math

import jax
import jax.numpy as jnp
import numpy as np
from jax import lax
from jax.experimental import pallas as pl
from jax.experimental.pallas import tpu as pltpu
from jax.sharding import PartitionSpec as P

NY = 2048
SCREEN_WEIGHT = 0.5
MESH = pl.DeviceIdType.MESH
LANES = 128
ROWS = 16
STRIDE = 27
CODE_MAX = 32767.0
TINY = 1e-30


def seed_tables(half):
    period = 8 * half
    unit = 2.0 * np.pi / period
    row = np.arange(ROWS)[:, None]
    lane = np.arange(LANES)[None, :]
    phases = []
    for p in range(2):
        phases.append((2 * row + p) * (2 * lane + 1))
    block = np.arange(half // ROWS)[:, None]
    phases.append(2 * ROWS * block * (2 * lane + 1))
    for p in range(2):
        for a in range(half // LANES):
            phases.append((2 * row + p) * (2 * LANES * a) + 0 * lane)
    phase = np.concatenate(phases, axis=0) % period
    return np.stack([np.cos(phase * unit), np.sin(phase * unit)]).astype(np.float32)


def small_sine(angle):
    square = angle * angle
    total = jnp.full_like(angle, 1.0 / 6227020800.0)
    for divisor in (-39916800.0, 362880.0, -5040.0, 120.0, -6.0, 1.0):
        total = total * square + 1.0 / divisor
    return total * angle


def split(value):
    high = value.astype(jnp.bfloat16)
    return high, (value - high.astype(jnp.float32)).astype(jnp.bfloat16)


def coded(value, axis):
    largest = jnp.maximum(jnp.max(jnp.abs(value), axis=axis, keepdims=True), TINY)
    codes = jnp.round(value * (CODE_MAX / largest)).astype(jnp.int32)
    return codes.astype(jnp.int16), largest * (1.0 / CODE_MAX)


def mixed(a, b, transposed=False):
    dims = (((1,), (1,)), ((), ())) if transposed else (((1,), (0,)), ((), ()))
    return lax.dot_general(a, b, dims, preferred_element_type=jnp.float32)


def kernel(
    gz, xy, chunks, w_ref, edge_ref, seed_ref, fx_ref, fy_ref, fz_ref, out_ref,
    fx, fy, fz, seeds, x_edge, code1, side1, got1, gotside1, table_hi, table_lo, planes,
    even, odd, code2, side2, got2, gotside2, lines, even_x, odd_x, factor,
    load_sem, edge_sem, sem1, sem2,
):
    g = lax.axis_index("gz")
    r = lax.axis_index("xy")
    depth = fx_ref.shape[1]
    nz = gz * depth
    half = nz // 2
    turn = min(256, half)
    f32 = jnp.float32

    loads = [
        pltpu.make_async_copy(src, dst, load_sem.at[i])
        for i, (src, dst) in enumerate(((fx_ref, fx), (fz_ref, fz), (fy_ref, fy), (seed_ref, seeds)))
    ]
    for load in loads:
        load.start()

    barrier = pltpu.get_barrier_semaphore()

    @pl.loop(1, gz)
    def _(i):
        pl.semaphore_signal(barrier, inc=1, device_id={"gz": lax.rem(g + i, gz)}, device_id_type=MESH)

    @pl.loop(1, xy)
    def _(i):
        pl.semaphore_signal(barrier, inc=1, device_id={"xy": lax.rem(r + i, xy)}, device_id_type=MESH)

    pl.semaphore_wait(barrier, gz + xy - 2)

    edge_copy = pltpu.make_async_remote_copy(
        src_ref=edge_ref, dst_ref=x_edge, send_sem=edge_sem.at[0], recv_sem=edge_sem.at[1],
        device_id={"xy": lax.rem(r + 1, xy)}, device_id_type=MESH,
    )

    @pl.when(r < xy - 1)
    def _():
        edge_copy.start()

    @pl.when(r == 0)
    def _():
        x_edge[...] = jnp.zeros_like(x_edge)

    for load in loads:
        load.wait()

    @pl.when(r > 0)
    def _():
        edge_copy.wait_recv()

    lane = lax.broadcasted_iota(jnp.int32, (depth, LANES), 1)
    plane = lax.broadcasted_iota(jnp.int32, (depth, LANES), 0)
    x_kept = (lane < LANES - 1) | (r < xy - 1)
    z_kept = (plane < depth - 1) | (g < gz - 1)
    edges = x_edge[...].astype(f32)

    @pl.loop(0, gz, unroll=4)
    def _(y):
        masked_x = jnp.where(x_kept, fx[y].astype(f32), 0.0)
        masked_z = jnp.where(z_kept, fz[y].astype(f32), 0.0)
        before = pltpu.roll(edges, lax.rem(LANES - y, LANES), 1)
        x_before = jnp.where(lane == 0, before, pltpu.roll(masked_x, 1, 1))
        z_before = jnp.where(plane == 0, 0.0, pltpu.roll(masked_z, 1, 0))
        slab = masked_x - x_before + w_ref[y] * fy[y].astype(f32) + masked_z - z_before
        codes, scale = coded(slab, 0)
        code1[y] = codes
        side1[y, :, :LANES] = scale
        side1[y, :, LANES:] = masked_z[depth - 1 :, :]

    def exchange1(peer):
        return (
            pltpu.make_async_remote_copy(
                src_ref=code1.at[peer], dst_ref=got1.at[g], send_sem=sem1.at[0], recv_sem=sem1.at[1],
                device_id={"gz": peer}, device_id_type=MESH,
            ),
            pltpu.make_async_remote_copy(
                src_ref=side1.at[peer], dst_ref=gotside1.at[g], send_sem=sem1.at[2], recv_sem=sem1.at[3],
                device_id={"gz": peer}, device_id_type=MESH,
            ),
        )

    @pl.loop(1, gz)
    def _(i):
        for copy in exchange1(lax.rem(g + i * STRIDE, gz)):
            copy.start()

    got1[g] = code1[g]
    gotside1[g] = side1[g]

    blocks = half // ROWS
    columns = half // LANES

    @pl.loop(0, blocks)
    def _(c):
        step_c = seeds[0, pl.ds(2 * ROWS + c, 1), :]
        step_s = seeds[1, pl.ds(2 * ROWS + c, 1), :]
        top = pl.multiple_of(c * ROWS, ROWS)
        for p in range(2):
            base_c = seeds[0, p * ROWS : (p + 1) * ROWS, :]
            base_s = seeds[1, p * ROWS : (p + 1) * ROWS, :]
            low_c = base_c * step_c - base_s * step_s
            low_s = base_s * step_c + base_c * step_s
            for a in range(columns):
                at = 2 * ROWS + blocks + (p * columns + a) * ROWS
                entry = seeds[0, at : at + ROWS, :] * low_c - seeds[1, at : at + ROWS, :] * low_s
                high, low = split(entry)
                table_hi[p, pl.ds(top, ROWS), a * LANES : (a + 1) * LANES] = high
                table_lo[p, pl.ds(top, ROWS), a * LANES : (a + 1) * LANES] = low

    across = lax.broadcasted_iota(jnp.int32, (turn, turn), 0) + lax.broadcasted_iota(jnp.int32, (turn, turn), 1)
    mirror = jnp.where(across == turn - 1, 1.0, 0.0).astype(jnp.bfloat16)

    def all_but_one(ref, sem):
        part = ref.at[pl.ds(0, ref.shape[0] - 1)]
        return pltpu.make_async_copy(part, part, sem)

    all_but_one(got1, sem1.at[1]).wait()
    all_but_one(gotside1, sem1.at[3]).wait()

    @pl.loop(0, gz, unroll=2)
    def _(k):
        value = got1[k].astype(jnp.int32).astype(f32) * gotside1[k, :, :LANES]
        below = gotside1[jnp.maximum(k - 1, 0), :, LANES:]
        value = value - jnp.where((plane == 0) & (k > 0), below, 0.0)
        high, low = split(value)
        at = pl.ds(pl.multiple_of(k * depth, depth), depth)
        planes[at, :LANES] = high
        planes[at, LANES:] = low

    for b in range(half // turn):
        here = slice(b * turn, (b + 1) * turn)
        there = slice(nz - (b + 1) * turn, nz - b * turn)
        lower = mixed(mirror, planes[there, :])
        lower = lower[:, :LANES] + lower[:, LANES:]
        upper = planes[here, :LANES].astype(f32) + planes[here, LANES:].astype(f32)
        even[here, :LANES], even[here, LANES:] = split(upper + lower)
        odd[here, :LANES], odd[here, LANES:] = split(upper - lower)

    def exchange2(peer):
        return (
            pltpu.make_async_remote_copy(
                src_ref=code2.at[peer], dst_ref=got2.at[r], send_sem=sem2.at[0], recv_sem=sem2.at[1],
                device_id={"xy": peer}, device_id_type=MESH,
            ),
            pltpu.make_async_remote_copy(
                src_ref=side2.at[peer], dst_ref=gotside2.at[r], send_sem=sem2.at[2], recv_sem=sem2.at[3],
                device_id={"xy": peer}, device_id_type=MESH,
            ),
        )

    chunk = half // chunks
    group = xy // chunks
    rows = half // xy

    @pl.loop(0, chunks)
    def _(c):
        at_chunk = lax.rem(r // group + chunks // 2 + c, chunks)
        here = pl.ds(pl.multiple_of(at_chunk * chunk, chunk), chunk)
        parts = []
        for p, folded in enumerate((even, odd)):
            wide = mixed(table_hi[p, here, :], folded[...])
            narrow = mixed(table_lo[p, here, :], folded[:, :LANES])
            parts.append(wide[:, :LANES] + wide[:, LANES:] + narrow)
        for j in range(group):
            peer = at_chunk * group + j
            block = jnp.concatenate([part[j * rows : (j + 1) * rows] for part in parts], axis=0)
            codes, scale = coded(block, 0)
            code2[peer] = codes
            side2[peer] = scale

            @pl.when(peer != r)
            def _():
                for copy in exchange2(peer):
                    copy.start()

    got2[r] = code2[r]
    gotside2[r] = side2[r]

    unit = math.pi / (2 * nz)
    at_row = lax.broadcasted_iota(jnp.int32, (2 * rows, LANES), 0)
    kz = 2 * rows * r + 2 * lax.rem(at_row, rows) + at_row // rows
    sine = small_sine(kz.astype(f32) * unit)
    weight = w_ref[g]
    base = 4.0 * sine * sine + weight * weight + SCREEN_WEIGHT
    gain = jnp.where(kz == 0, -math.sqrt(0.5), -1.0) * (2.0 / nz)
    for p in range(2):
        for a in range(columns):
            kx = 2 * (lax.broadcasted_iota(jnp.int32, (1, LANES), 1) + a * LANES) + p
            sine = small_sine(kx.astype(f32) * unit)
            own = jnp.where(kx == 0, math.sqrt(0.5), 1.0)
            at = (p * columns + a) * LANES
            factor[:, at : at + LANES] = gain * own / (base + 4.0 * sine * sine)

    all_but_one(got2, sem2.at[1]).wait()
    all_but_one(gotside2, sem2.at[3]).wait()

    tall = 2 * rows
    for k in range(xy):
        value = got2[k].astype(jnp.int32).astype(f32) * gotside2[k]
        high, low = split(value)
        lines[:tall, k * LANES : (k + 1) * LANES] = high
        lines[tall:, k * LANES : (k + 1) * LANES] = low

    for b in range(half // turn):
        here = slice(b * turn, (b + 1) * turn)
        there = slice(nz - (b + 1) * turn, nz - b * turn)
        lower = mixed(lines[:, there], mirror)
        lower = lower[:tall] + lower[tall:]
        upper = lines[:tall, here].astype(f32) + lines[tall:, here].astype(f32)
        even_x[:tall, here], even_x[tall:, here] = split(upper + lower)
        odd_x[:tall, here], odd_x[tall:, here] = split(upper - lower)

    for p, folded in enumerate((even_x, odd_x)):
        for b in range(half // turn):
            here = slice(b * turn, (b + 1) * turn)
            wide = mixed(folded[...], table_hi[p, here, :], True)
            narrow = mixed(folded[:tall, :], table_lo[p, here, :], True)
            at = p * half + b * turn
            total = wide[:tall] + wide[tall:] + narrow
            out_ref[:, at : at + turn] = total * factor[:, at : at + turn]

    @pl.when(r < xy - 1)
    def _():
        edge_copy.wait_send()

    for ref, sem in ((code1, sem1.at[0]), (side1, sem1.at[2]), (code2, sem2.at[0]), (side2, sem2.at[2])):
        all_but_one(ref, sem).wait()


def shards(gz, xy, flux_xface, flux_yspec, flux_zface, frequency_y):
    rows_y, depth, width = flux_xface.shape
    nz = gz * depth
    half = nz // 2
    tall = nz // xy
    chunks = 4 if xy >= 8 else 2
    weight_y = 2.0 * jnp.sin(frequency_y.astype(jnp.float32) * (math.pi / (2 * NY)))
    weight = jnp.broadcast_to(weight_y[:, None, None], (rows_y, 1, LANES))
    edge = jnp.pad(flux_xface[:, :, width - 1].T, ((0, 0), (0, LANES - rows_y)))
    seeds = jnp.asarray(seed_tables(half))
    bf16, f32, i16 = jnp.bfloat16, jnp.float32, jnp.int16
    vmem = pl.BlockSpec(memory_space=pltpu.VMEM)
    hbm = pl.BlockSpec(memory_space=pl.ANY)
    slab = (rows_y, depth, LANES)
    result = pl.pallas_call(
        functools.partial(kernel, gz, xy, chunks),
        out_shape=jax.ShapeDtypeStruct((tall, nz), f32),
        in_specs=[vmem, vmem, hbm, hbm, hbm, hbm],
        out_specs=vmem,
        scratch_shapes=[
            pltpu.VMEM(slab, bf16),
            pltpu.VMEM(slab, bf16),
            pltpu.VMEM(slab, bf16),
            pltpu.VMEM(seeds.shape, f32),
            pltpu.VMEM((depth, LANES), bf16),
            pltpu.VMEM(slab, i16),
            pltpu.VMEM((rows_y, 1, 2 * LANES), f32),
            pltpu.VMEM(slab, i16),
            pltpu.VMEM((rows_y, 1, 2 * LANES), f32),
            pltpu.VMEM((2, half, half), bf16),
            pltpu.VMEM((2, half, half), bf16),
            pltpu.VMEM((nz, 2 * LANES), bf16),
            pltpu.VMEM((half, 2 * LANES), bf16),
            pltpu.VMEM((half, 2 * LANES), bf16),
            pltpu.VMEM((xy, tall, LANES), i16),
            pltpu.VMEM((xy, 1, LANES), f32),
            pltpu.VMEM((xy, tall, LANES), i16),
            pltpu.VMEM((xy, 1, LANES), f32),
            pltpu.VMEM((2 * tall, nz), bf16),
            pltpu.VMEM((2 * tall, half), bf16),
            pltpu.VMEM((2 * tall, half), bf16),
            pltpu.VMEM((tall, nz), f32),
            pltpu.SemaphoreType.DMA((4,)),
            pltpu.SemaphoreType.DMA((2,)),
            pltpu.SemaphoreType.DMA((4,)),
            pltpu.SemaphoreType.DMA((4,)),
        ],
        compiler_params=pltpu.CompilerParams(
            collective_id=0, has_side_effects=True, vmem_limit_bytes=48 * 1024 * 1024
        ),
    )(weight, edge, seeds, flux_xface, flux_yspec, flux_zface)
    spread = result.reshape(2, tall // 2, 2, half).transpose(1, 0, 2, 3)
    return spread.reshape(1, tall, 2, half)


def solution(mesh):
    return jax.shard_map(
        functools.partial(shards, mesh.shape["gz"], mesh.shape["xy"]),
        mesh=mesh,
        in_specs=(P(None, "gz", "xy"), P(None, "gz", "xy"), P(None, "gz", "xy"), P()),
        out_specs=P("gz", "xy", None, None),
        check_vma=False,
    )
```

time: 215 us -> 72.8 us (0.34)
  the two profiles are of different devices: /device:TPU:18 before, /device:TPU:2 now
where the time goes in v1:
time: 72.8 us; the launch traced here: 72.5 us
  Pallas kernels  66.2 us (91%)
  local copies, waits for them, and re-layouts  5.49 us (8%)
    pallas_call x1, Pallas kernels, shards(): pl.pallas_call(functools.partial(kernel, gz, xy, chunks), out_shape=jax.S...  66.2 us
    unnamed x9, local copies, waits for them, and re-layouts  2.01 us

profile of v1, /device:TPU:2, one launch (start us, length us, event | category | flops | bytes accessed | tf_op | source)
XLA Modules:
  0.0 72.5 jit_solution(3000572155753205800)
XLA Ops:
  0.0 0.7 sine_multiply_fusion
  0.7 0.1 broadcast_in_dim.2.w_ref
  0.8 0.0 copy-start.1
  0.8 0.0 copy-start.2
  0.9 1.3 %slice.3 = bf16[64,32,1]{2,1,0:T(8,128)(2,1)S(1)} slice(bf16[64,32,128]{2,1,0:T(8,128)(2,1)} %fx_ref.1), slice={[0:64], [0:32], [127:128]} | slice | bytes 8192 | tf_op jit(solution)/shard_map/slice | solution.py:303
  2.2 0.0 copy-start
  2.2 0.6 copy.8
  2.8 0.0 copy-done.1
  2.8 0.0 copy-done.2
  2.9 0.4 copy-done
  3.2 0.0 copy-start.3
  3.2 1.0 %copy-done.3 = f32[2,352,128]{2,1,0:T(8,128)S(1)} copy-done((f32[2,352,128]{2,1,0:T(8,128)S(1)}, f32[2,352,128]{2,1,0:T(8,128)}, u32[]{:S(2)}) %copy-start.3) | copy-done | bytes 360472
  4.2 66.2 %shard_map.55 = f32[128,2048]{1,0:T(8,128)S(1)} custom-call(f32[64,1,128]{2,1,0:T(1,128)S(1)} %broadcast_in_dim.2.w_ref, bf16[32,128]{1,0:T(8,128)(2,1)S(1)} %pad.4.edge_ref, f32[2,352,128]{2,1,0:T(8,128)S(1)} %copy-done.3, bf16[64,32,128]{2,1,0:T(8,128)(2,1)S(1)} %copy-done, bf16[64,32,128]{2,1,0:T(8,128)(2,1)S(1)} %copy-done.1, ...), custom_call_target="tpu_custom_call" | custom-call | tf_op jit(solution)/shard_map/pallas_call | solution.py:309
  70.5 0.9 %reshape.9 = f32[2,64,2,1024]{3,2,1,0:T(2,128)S(1)} reshape(f32[128,2048]{1,0:T(8,128)S(1)} %shard_map.55) | data formatting | bytes 2097152 | tf_op jit(solution)/shard_map/reshape | solution.py:346
  71.4 1.1 %copy.7 = f32[64,2,2,1024]{3,2,1,0:T(2,128)} copy(f32[64,2,2,1024]{3,2,0,1:T(2,128)S(1)} %bitcast.5) | data formatting | bytes 2097152 | tf_op jit(solution)/shard_map/transpose | solution.py:346
  (1 shorter events, 0.0 us)
Async XLA Ops:
  0.8 2.0 %copy-start.1 = (bf16[64,32,128]{2,1,0:T(8,128)(2,1)S(1)}, bf16[64,32,128]{2,1,0:T(8,128)(2,1)}, u32[]{:S(2)}) copy-start(bf16[64,32,128]{2,1,0:T(8,128)(2,1)} %fy_ref.1) | copy-start | bytes 1572868
  0.8 2.0 %copy-start.2 = (bf16[64,32,128]{2,1,0:T(8,128)(2,1)S(1)}, bf16[64,32,128]{2,1,0:T(8,128)(2,1)}, u32[]{:S(2)}) copy-start(bf16[64,32,128]{2,1,0:T(8,128)(2,1)} %fz_ref.1) | copy-start | bytes 1572868
  2.2 1.0 %copy-start = (bf16[64,32,128]{2,1,0:T(8,128)(2,1)S(1)}, bf16[64,32,128]{2,1,0:T(8,128)(2,1)}, u32[]{:S(2)}) copy-start(bf16[64,32,128]{2,1,0:T(8,128)(2,1)} %fx_ref.1) | copy-start | bytes 1572868
  3.2 1.0 %copy-start.3 = (f32[2,352,128]{2,1,0:T(8,128)S(1)}, f32[2,352,128]{2,1,0:T(8,128)}, u32[]{:S(2)}) copy-start(f32[2,352,128]{2,1,0:T(8,128)} %constant.9.clone.seed_ref) | copy-start | bytes 1081348

commit v2 on v1

v2 whole, which is shorter than its diff:
```python
import functools
import math

import jax
import jax.numpy as jnp
import numpy as np
from jax import lax
from jax.experimental import pallas as pl
from jax.experimental.pallas import tpu as pltpu
from jax.sharding import PartitionSpec as P

NY = 2048
SCREEN_WEIGHT = 0.5
MESH = pl.DeviceIdType.MESH
LANES = 128
ROWS = 16
STRIDE = 27
CODE_MAX = 32767.0
TINY = 1e-30


def seed_tables(half):
    period = 8 * half
    unit = 2.0 * np.pi / period
    row = np.arange(ROWS)[:, None]
    lane = np.arange(LANES)[None, :]
    phases = []
    for p in range(2):
        phases.append((2 * row + p) * (2 * lane + 1))
    block = np.arange(half // ROWS)[:, None]
    phases.append(2 * ROWS * block * (2 * lane + 1))
    for p in range(2):
        for a in range(half // LANES):
            phases.append((2 * row + p) * (2 * LANES * a) + 0 * lane)
    phase = np.concatenate(phases, axis=0) % period
    return np.stack([np.cos(phase * unit), np.sin(phase * unit)]).astype(np.float32)


def small_sine(angle):
    square = angle * angle
    total = jnp.full_like(angle, 1.0 / 6227020800.0)
    for divisor in (-39916800.0, 362880.0, -5040.0, 120.0, -6.0, 1.0):
        total = total * square + 1.0 / divisor
    return total * angle


def split(value):
    high = value.astype(jnp.bfloat16)
    return high, (value - high.astype(jnp.float32)).astype(jnp.bfloat16)


def coded(value, axis):
    largest = jnp.maximum(jnp.max(jnp.abs(value), axis=axis, keepdims=True), TINY)
    codes = jnp.round(value * (CODE_MAX / largest)).astype(jnp.int32)
    return codes.astype(jnp.int16), largest * (1.0 / CODE_MAX)


def mixed(a, b, transposed=False):
    dims = (((1,), (1,)), ((), ())) if transposed else (((1,), (0,)), ((), ()))
    return lax.dot_general(a, b, dims, preferred_element_type=jnp.float32)


def kernel(
    gz, xy, chunks, frequency_ref, seed_ref, fx_ref, fy_ref, fz_ref, out_ref,
    fx, fy, fz, seeds, weights, page, edge_out, edge_in, code1, side1, got1, gotside1, gotedge,
    table_hi, table_lo, planes, even, odd, code2, side2, got2, gotside2, factor, sums,
    load_sem, edge_sem, send1, recv1, send2, recv2,
):
    g = lax.axis_index("gz")
    r = lax.axis_index("xy")
    depth = fx_ref.shape[1]
    nz = gz * depth
    half = nz // 2
    turn = min(256, half)
    f32 = jnp.float32

    barrier = pltpu.get_barrier_semaphore()

    @pl.loop(1, gz, unroll=7)
    def _(i):
        peer = lax.rem(g + i * STRIDE, gz)
        pl.semaphore_signal(barrier, inc=1, device_id={"gz": peer}, device_id_type=MESH)

    for i in range(1, xy):
        peer = lax.rem(r + i, xy)
        pl.semaphore_signal(barrier, inc=1, device_id={"xy": peer}, device_id_type=MESH)

    loads = [
        pltpu.make_async_copy(src, dst, load_sem.at[i])
        for i, (src, dst) in enumerate(((fx_ref, fx), (fz_ref, fz), (fy_ref, fy), (seed_ref, seeds)))
    ]
    for load in loads:
        load.start()

    for y in range(gz):
        weights[y : y + 1, :] = jnp.full((1, LANES), frequency_ref[y].astype(f32))
    weights[...] = 2.0 * small_sine(weights[...] * (math.pi / (2 * NY)))

    for load in loads:
        load.wait()

    lane = lax.broadcasted_iota(jnp.int32, (depth, LANES), 1)
    plane = lax.broadcasted_iota(jnp.int32, (depth, LANES), 0)
    x_kept = (lane < LANES - 1) | (r < xy - 1)
    z_kept = (plane < depth - 1) | (g < gz - 1)

    def slab_of(y, edge):
        masked_x = jnp.where(x_kept, fx[y].astype(f32), 0.0)
        masked_z = jnp.where(z_kept, fz[y].astype(f32), 0.0)
        x_before = jnp.where(lane == 0, 0.0, pltpu.roll(masked_x, 1, 1))
        z_before = jnp.where(plane == 0, 0.0, pltpu.roll(masked_z, 1, 0))
        weight = weights[pl.ds(y, 1), :]
        slab = masked_x - x_before + weight * fy[y].astype(f32) + masked_z - z_before
        largest = jnp.maximum(jnp.max(jnp.abs(slab), axis=0, keepdims=True), TINY)
        scale = (largest * (1.01 / CODE_MAX)).astype(jnp.bfloat16).astype(f32)
        code1[y] = jnp.round(slab / scale).astype(jnp.int32).astype(jnp.int16)
        side1[y, 0:1, :] = scale.astype(jnp.bfloat16)
        side1[y, 1:2, :] = masked_z[depth - 1 :, :].astype(jnp.bfloat16)
        return jnp.where(lane == y, pltpu.roll(masked_x, lax.rem(y + 1, LANES), 1), edge)

    edge = lax.fori_loop(0, gz, slab_of, jnp.zeros((depth, LANES), f32), unroll=4)
    wide = jnp.concatenate([edge, jnp.zeros((LANES - depth, LANES), f32)], axis=0)
    page[...] = wide.T

    @pl.loop(0, gz, unroll=4)
    def _(y):
        edge_out[y] = page[pl.ds(y, 1), :]

    pl.semaphore_wait(barrier, gz + xy - 2)

    edge_copy = pltpu.make_async_remote_copy(
        src_ref=edge_out, dst_ref=edge_in, send_sem=edge_sem.at[0], recv_sem=edge_sem.at[1],
        device_id={"xy": lax.rem(r + 1, xy)}, device_id_type=MESH,
    )

    @pl.when(r < xy - 1)
    def _():
        edge_copy.start()

    def exchange1(source, target, which, peer):
        return pltpu.make_async_remote_copy(
            src_ref=source.at[peer], dst_ref=target.at[g], send_sem=send1.at[which], recv_sem=recv1.at[which],
            device_id={"gz": peer}, device_id_type=MESH,
        )

    @pl.loop(1, gz)
    def _(i):
        peer = lax.rem(g + i * STRIDE, gz)
        exchange1(code1, got1, 0, peer).start()
        exchange1(side1, gotside1, 1, peer).start()

    got1[g] = code1[g]
    gotside1[g] = side1[g]

    @pl.when(r > 0)
    def _():
        edge_copy.wait_recv()

        @pl.loop(1, gz)
        def _(i):
            exchange1(edge_in, gotedge, 2, lax.rem(g + i * STRIDE, gz)).start()

        gotedge[g] = edge_in[g]

    blocks = half // ROWS
    columns = half // LANES

    @pl.loop(0, blocks)
    def _(c):
        step_c = seeds[0, pl.ds(2 * ROWS + c, 1), :]
        step_s = seeds[1, pl.ds(2 * ROWS + c, 1), :]
        top = pl.multiple_of(c * ROWS, ROWS)
        for p in range(2):
            base_c = seeds[0, p * ROWS : (p + 1) * ROWS, :]
            base_s = seeds[1, p * ROWS : (p + 1) * ROWS, :]
            low_c = base_c * step_c - base_s * step_s
            low_s = base_s * step_c + base_c * step_s
            for a in range(columns):
                at = 2 * ROWS + blocks + (p * columns + a) * ROWS
                entry = seeds[0, at : at + ROWS, :] * low_c - seeds[1, at : at + ROWS, :] * low_s
                high, low = split(entry)
                table_hi[p, pl.ds(top, ROWS), a * LANES : (a + 1) * LANES] = high
                table_lo[p, pl.ds(top, ROWS), a * LANES : (a + 1) * LANES] = low

    across = lax.broadcasted_iota(jnp.int32, (turn, turn), 0) + lax.broadcasted_iota(jnp.int32, (turn, turn), 1)
    mirror = jnp.where(across == turn - 1, 1.0, 0.0).astype(jnp.bfloat16)

    rows = half // xy
    tall = 2 * rows
    unit = math.pi / (2 * nz)
    at_row = lax.broadcasted_iota(jnp.int32, (tall, LANES), 0)
    kz = tall * r + 2 * lax.rem(at_row, rows) + at_row // rows
    sine = small_sine(kz.astype(f32) * unit)
    weight = weights[pl.ds(g, 1), :]
    base = 4.0 * sine * sine + weight * weight + SCREEN_WEIGHT
    gain = jnp.where(kz == 0, -math.sqrt(0.5), -1.0) * (2.0 / nz)
    for p in range(2):
        for a in range(columns):
            kx = 2 * (lax.broadcasted_iota(jnp.int32, (1, LANES), 1) + a * LANES) + p
            sine = small_sine(kx.astype(f32) * unit)
            own = jnp.where(kx == 0, math.sqrt(0.5), 1.0)
            at = (p * columns + a) * LANES
            factor[:, at : at + LANES] = gain * own / (base + 4.0 * sine * sine)

    def all_but_one(ref, sem):
        part = ref.at[pl.ds(0, ref.shape[0] - 1)]
        return pltpu.make_async_copy(part, part, sem)

    @pl.when(r == 0)
    def _():
        gotedge[...] = jnp.zeros_like(gotedge)

    @pl.when(r > 0)
    def _():
        all_but_one(gotedge, recv1.at[2]).wait()

    page[...] = jnp.zeros_like(page)

    @pl.loop(0, gz, unroll=4)
    def _(k):
        page[pl.ds(k, 1), :] = gotedge[k]

    edges = page[...].T[:depth]

    all_but_one(gotside1, recv1.at[1]).wait()
    all_but_one(got1, recv1.at[0]).wait()

    @pl.loop(0, gz, unroll=2)
    def _(k):
        value = got1[k].astype(jnp.int32).astype(f32) * gotside1[k, 0:1, :].astype(f32)
        below = gotside1[jnp.maximum(k - 1, 0), 1:2, :].astype(f32)
        value = value - jnp.where((plane == 0) & (k > 0), below, 0.0)
        value = value - jnp.where(lane == 0, pltpu.roll(edges, lax.rem(LANES - k, LANES), 1), 0.0)
        high, low = split(value)
        at = pl.ds(pl.multiple_of(k * depth, depth), depth)
        planes[at, :LANES] = high
        planes[at, LANES:] = low

    for b in range(half // turn):
        here = slice(b * turn, (b + 1) * turn)
        there = slice(nz - (b + 1) * turn, nz - b * turn)
        lower = mixed(mirror, planes[there, :])
        lower = lower[:, :LANES] + lower[:, LANES:]
        upper = planes[here, :LANES].astype(f32) + planes[here, LANES:].astype(f32)
        even[here, :LANES], even[here, LANES:] = split(upper + lower)
        odd[here, :LANES], odd[here, LANES:] = split(upper - lower)

    def exchange2(source, target, which, peer):
        return pltpu.make_async_remote_copy(
            src_ref=source.at[peer], dst_ref=target.at[r], send_sem=send2.at[which], recv_sem=recv2.at[which, r],
            device_id={"xy": peer}, device_id_type=MESH,
        )

    chunk = half // chunks
    group = xy // chunks

    @pl.loop(0, chunks)
    def _(c):
        at_chunk = lax.rem(r // group + chunks // 2 + c, chunks)
        here = pl.ds(pl.multiple_of(at_chunk * chunk, chunk), chunk)
        parts = []
        for p, folded in enumerate((even, odd)):
            wide = mixed(table_hi[p, here, :], folded[...])
            narrow = mixed(table_lo[p, here, :], folded[:, :LANES])
            parts.append(wide[:, :LANES] + wide[:, LANES:] + narrow)
        for j in range(group):
            peer = at_chunk * group + j
            block = jnp.concatenate([part[j * rows : (j + 1) * rows] for part in parts], axis=0)
            codes, scale = coded(block, 0)
            code2[peer] = codes
            side2[peer] = scale

            @pl.when(peer != r)
            def _():
                exchange2(code2, got2, 0, peer).start()
                exchange2(side2, gotside2, 1, peer).start()

    got2[r] = code2[r]
    gotside2[r] = side2[r]

    pair = turn // LANES
    steps = half // turn

    def line_block(first):
        parts = []
        for i in range(pair):
            source = first + i

            @pl.when(source != r)
            def _():
                pltpu.make_async_copy(got2.at[source], got2.at[source], recv2.at[0, source]).wait()
                pltpu.make_async_copy(gotside2.at[source], gotside2.at[source], recv2.at[1, source]).wait()

            parts.append(got2[source].astype(jnp.int32).astype(f32) * gotside2[source])
        return jnp.concatenate(parts, axis=1)

    start = jnp.where(2 * r < xy, steps // 2, 0)
    for i in range(steps):
        b = lax.rem(start + i, steps)
        upper = line_block(b * pair)
        far = jnp.concatenate(split(line_block(xy - (b + 1) * pair)), axis=0)
        lower = mixed(far, mirror)
        lower = lower[:tall] + lower[tall:]
        here = pl.ds(pl.multiple_of(b * turn, turn), turn)
        for p, value in enumerate((upper + lower, upper - lower)):
            folded = jnp.concatenate(split(value), axis=0)
            for t in range(half // turn):
                entries = slice(t * turn, (t + 1) * turn)
                wide = mixed(folded, table_hi[p, entries, here], True)
                narrow = mixed(folded[:tall], table_lo[p, entries, here], True)
                total = wide[:tall] + wide[tall:] + narrow
                at = p * half + t * turn
                if i > 0:
                    total = total + sums[:, at : at + turn]
                if i < steps - 1:
                    sums[:, at : at + turn] = total
                    continue
                total = total * factor[:, at : at + turn]
                for z in range(2):
                    for a in range(pair):
                        row = z * 2 * columns + 2 * (t * pair + a) + p
                        out_ref[pl.ds(row, rows, stride=4 * columns), :] = total[
                            z * rows : (z + 1) * rows, a * LANES : (a + 1) * LANES
                        ]

    @pl.when(r < xy - 1)
    def _():
        edge_copy.wait_send()

    @pl.when(r > 0)
    def _():
        all_but_one(edge_in, send1.at[2]).wait()

    for ref, sem in ((code1, send1.at[0]), (side1, send1.at[1]), (code2, send2.at[0]), (side2, send2.at[1])):
        all_but_one(ref, sem).wait()


def shards(gz, xy, flux_xface, flux_yspec, flux_zface, frequency_y):
    rows_y, depth, width = flux_xface.shape
    nz = gz * depth
    half = nz // 2
    tall = nz // xy
    columns = half // LANES
    chunks = 4 if xy >= 8 else 2
    seeds = jnp.asarray(seed_tables(half))
    bf16, f32, i16 = jnp.bfloat16, jnp.float32, jnp.int16
    hbm = pl.BlockSpec(memory_space=pl.ANY)
    slab = (rows_y, depth, LANES)
    result = pl.pallas_call(
        functools.partial(kernel, gz, xy, chunks),
        out_shape=jax.ShapeDtypeStruct((tall * 2 * columns, LANES), f32),
        in_specs=[pl.BlockSpec(memory_space=pltpu.SMEM), hbm, hbm, hbm, hbm],
        out_specs=pl.BlockSpec(memory_space=pltpu.VMEM),
        scratch_shapes=[
            pltpu.VMEM(slab, bf16),
            pltpu.VMEM(slab, bf16),
            pltpu.VMEM(slab, bf16),
            pltpu.VMEM(seeds.shape, f32),
            pltpu.VMEM((rows_y, LANES), f32),
            pltpu.VMEM((LANES, LANES), f32),
            pltpu.VMEM((rows_y, 1, LANES), f32),
            pltpu.VMEM((rows_y, 1, LANES), f32),
            pltpu.VMEM(slab, i16),
            pltpu.VMEM((rows_y, 2, LANES), bf16),
            pltpu.VMEM(slab, i16),
            pltpu.VMEM((rows_y, 2, LANES), bf16),
            pltpu.VMEM((rows_y, 1, LANES), f32),
            pltpu.VMEM((2, half, half), bf16),
            pltpu.VMEM((2, half, half), bf16),
            pltpu.VMEM((nz, 2 * LANES), bf16),
            pltpu.VMEM((half, 2 * LANES), bf16),
            pltpu.VMEM((half, 2 * LANES), bf16),
            pltpu.VMEM((xy, tall, LANES), i16),
            pltpu.VMEM((xy, 1, LANES), f32),
            pltpu.VMEM((xy, tall, LANES), i16),
            pltpu.VMEM((xy, 1, LANES), f32),
            pltpu.VMEM((tall, nz), f32),
            pltpu.VMEM((tall, nz), f32),
            pltpu.SemaphoreType.DMA((4,)),
            pltpu.SemaphoreType.DMA((2,)),
            pltpu.SemaphoreType.DMA((3,)),
            pltpu.SemaphoreType.DMA((3,)),
            pltpu.SemaphoreType.DMA((2,)),
            pltpu.SemaphoreType.DMA((2, xy)),
        ],
        compiler_params=pltpu.CompilerParams(
            collective_id=0, has_side_effects=True, vmem_limit_bytes=60 * 1024 * 1024
        ),
    )(frequency_y, seeds, flux_xface, flux_yspec, flux_zface)
    spread = result.reshape(tall, columns, 2, LANES).transpose(0, 2, 1, 3)
    return spread.reshape(1, tall, 2, half)


def solution(mesh):
    return jax.shard_map(
        functools.partial(shards, mesh.shape["gz"], mesh.shape["xy"]),
        mesh=mesh,
        in_specs=(P(None, "gz", "xy"), P(None, "gz", "xy"), P(None, "gz", "xy"), P()),
        out_specs=P("gz", "xy", None, None),
        check_vma=False,
    )
```

time: 72.8 us -> 68.7 us (0.944)
  the two profiles are of different devices: /device:TPU:2 before, /device:TPU:14 now
where the time goes in v2:
time: 68.7 us; the launch traced here: 68.5 us
  Pallas kernels  66.2 us (96%)
  local copies, waits for them, and re-layouts  2.26 us (3%)
    pallas_call x1, Pallas kernels, shards(): pl.pallas_call(functools.partial(kernel, gz, xy, chunks), out_shape=jax.S...  66.2 us
    unnamed x1, local copies, waits for them, and re-layouts  2.26 us

profile of v2, /device:TPU:14, one launch (start us, length us, event | category | flops | bytes accessed | tf_op | source)
XLA Modules:
  0.0 68.5 jit_solution(17527950080588817288)
XLA Ops:
  0.0 66.2 %shard_map.55 = f32[2048,128]{1,0:T(8,128)} custom-call(s32[64]{0:T(128)} %frequency_ref.1, f32[2,352,128]{2,1,0:T(8,128)} %constant.2.clone.seed_ref, bf16[64,32,128]{2,1,0:T(8,128)(2,1)} %fx_ref.1, bf16[64,32,128]{2,1,0:T(8,128)(2,1)} %fy_ref.1, bf16[64,32,128]{2,1,0:T(8,128)(2,1)} %fz_ref.1), custom_call_target="tpu_custom_call" | custom-call | tf_op jit(solution)/shard_map/pallas_call | solution.py:349
  66.2 2.3 %copy.8 = f32[1,128,2,1024]{3,2,1,0:T(2,128)} copy(f32[1,128,2,1024]{3,2,1,0:T(2,128)} %bitcast.5) | data formatting | bytes 2097152

commit v3 on v2

--- a/solution.py
+++ b/solution.py
@@ -64,7 +64,7 @@
     gz, xy, chunks, frequency_ref, seed_ref, fx_ref, fy_ref, fz_ref, out_ref,
     fx, fy, fz, seeds, weights, page, edge_out, edge_in, code1, side1, got1, gotside1, gotedge,
     table_hi, table_lo, planes, even, odd, code2, side2, got2, gotside2, factor, sums,
-    load_sem, edge_sem, send1, recv1, send2, recv2,
+    frequency, load_sem, edge_sem, send1, recv1, send2, recv2,
 ):
     g = lax.axis_index("gz")
     r = lax.axis_index("xy")
@@ -74,6 +74,13 @@
     turn = min(256, half)
     f32 = jnp.float32
 
+    loads = [
+        pltpu.make_async_copy(src, dst, load_sem.at[i])
+        for i, (src, dst) in enumerate(((frequency_ref, frequency), (fx_ref, fx), (fz_ref, fz), (fy_ref, fy), (seed_ref, seeds)))
+    ]
+    for load in loads:
+        load.start()
+
     barrier = pltpu.get_barrier_semaphore()
 
     @pl.loop(1, gz, unroll=7)
@@ -85,18 +92,12 @@
         peer = lax.rem(r + i, xy)
         pl.semaphore_signal(barrier, inc=1, device_id={"xy": peer}, device_id_type=MESH)
 
-    loads = [
-        pltpu.make_async_copy(src, dst, load_sem.at[i])
-        for i, (src, dst) in enumerate(((fx_ref, fx), (fz_ref, fz), (fy_ref, fy), (seed_ref, seeds)))
-    ]
-    for load in loads:
-        load.start()
-
+    loads[0].wait()
     for y in range(gz):
-        weights[y : y + 1, :] = jnp.full((1, LANES), frequency_ref[y].astype(f32))
+        weights[y : y + 1, :] = jnp.full((1, LANES), frequency[y].astype(f32))
     weights[...] = 2.0 * small_sine(weights[...] * (math.pi / (2 * NY)))
 
-    for load in loads:
+    for load in loads[1:4]:
         load.wait()
 
     lane = lax.broadcasted_iota(jnp.int32, (depth, LANES), 1)
@@ -113,12 +114,12 @@
         slab = masked_x - x_before + weight * fy[y].astype(f32) + masked_z - z_before
         largest = jnp.maximum(jnp.max(jnp.abs(slab), axis=0, keepdims=True), TINY)
         scale = (largest * (1.01 / CODE_MAX)).astype(jnp.bfloat16).astype(f32)
-        code1[y] = jnp.round(slab / scale).astype(jnp.int32).astype(jnp.int16)
+        code1[y] = jnp.round(slab * (1.0 / scale)).astype(jnp.int32).astype(jnp.int16)
         side1[y, 0:1, :] = scale.astype(jnp.bfloat16)
         side1[y, 1:2, :] = masked_z[depth - 1 :, :].astype(jnp.bfloat16)
         return jnp.where(lane == y, pltpu.roll(masked_x, lax.rem(y + 1, LANES), 1), edge)
 
-    edge = lax.fori_loop(0, gz, slab_of, jnp.zeros((depth, LANES), f32), unroll=4)
+    edge = lax.fori_loop(0, gz, slab_of, jnp.zeros((depth, LANES), f32), unroll=8)
     wide = jnp.concatenate([edge, jnp.zeros((LANES - depth, LANES), f32)], axis=0)
     page[...] = wide.T
 
@@ -162,6 +163,7 @@
 
         gotedge[g] = edge_in[g]
 
+    loads[4].wait()
     blocks = half // ROWS
     columns = half // LANES
 
@@ -225,7 +227,7 @@
     all_but_one(gotside1, recv1.at[1]).wait()
     all_but_one(got1, recv1.at[0]).wait()
 
-    @pl.loop(0, gz, unroll=2)
+    @pl.loop(0, gz, unroll=8)
     def _(k):
         value = got1[k].astype(jnp.int32).astype(f32) * gotside1[k, 0:1, :].astype(f32)
         below = gotside1[jnp.maximum(k - 1, 0), 1:2, :].astype(f32)
@@ -269,6 +271,8 @@
             codes, scale = coded(block, 0)
             code2[peer] = codes
             side2[peer] = scale
+        for j in range(group):
+            peer = at_chunk * group + lax.rem(r + j, group)
 
             @pl.when(peer != r)
             def _():
@@ -335,6 +339,12 @@
         all_but_one(ref, sem).wait()
 
 
+def put_out(held_ref, out_ref, sem):
+    copy = pltpu.make_async_copy(held_ref, out_ref, sem)
+    copy.start()
+    copy.wait()
+
+
 def shards(gz, xy, flux_xface, flux_yspec, flux_zface, frequency_y):
     rows_y, depth, width = flux_xface.shape
     nz = gz * depth
@@ -344,13 +354,14 @@
     chunks = 4 if xy >= 8 else 2
     seeds = jnp.asarray(seed_tables(half))
     bf16, f32, i16 = jnp.bfloat16, jnp.float32, jnp.int16
-    hbm = pl.BlockSpec(memory_space=pl.ANY)
+    hbm = pl.BlockSpec(memory_space=pltpu.HBM)
+    vmem = pl.BlockSpec(memory_space=pltpu.VMEM)
     slab = (rows_y, depth, LANES)
     result = pl.pallas_call(
         functools.partial(kernel, gz, xy, chunks),
         out_shape=jax.ShapeDtypeStruct((tall * 2 * columns, LANES), f32),
-        in_specs=[pl.BlockSpec(memory_space=pltpu.SMEM), hbm, hbm, hbm, hbm],
-        out_specs=pl.BlockSpec(memory_space=pltpu.VMEM),
+        in_specs=[hbm] * 5,
+        out_specs=vmem,
         scratch_shapes=[
             pltpu.VMEM(slab, bf16),
             pltpu.VMEM(slab, bf16),
@@ -376,7 +387,8 @@
             pltpu.VMEM((xy, 1, LANES), f32),
             pltpu.VMEM((tall, nz), f32),
             pltpu.VMEM((tall, nz), f32),
-            pltpu.SemaphoreType.DMA((4,)),
+            pltpu.SMEM((rows_y,), jnp.int32),
+            pltpu.SemaphoreType.DMA((5,)),
             pltpu.SemaphoreType.DMA((2,)),
             pltpu.SemaphoreType.DMA((3,)),
             pltpu.SemaphoreType.DMA((3,)),
@@ -384,9 +396,17 @@
             pltpu.SemaphoreType.DMA((2, xy)),
         ],
         compiler_params=pltpu.CompilerParams(
-            collective_id=0, has_side_effects=True, vmem_limit_bytes=60 * 1024 * 1024
+            collective_id=0, has_side_effects=True, vmem_limit_bytes=24 * 1024 * 1024
         ),
-    )(frequency_y, seeds, flux_xface, flux_yspec, flux_zface)
+    )(*(pltpu.with_memory_space_constraint(a, pltpu.HBM) for a in (frequency_y, seeds, flux_xface, flux_yspec, flux_zface)))
+    result = pl.pallas_call(
+        put_out,
+        out_shape=jax.ShapeDtypeStruct(result.shape, f32),
+        in_specs=[vmem],
+        out_specs=hbm,
+        scratch_shapes=[pltpu.SemaphoreType.DMA],
+        compiler_params=pltpu.CompilerParams(vmem_limit_bytes=1024 * 1024),
+    )(result)
     spread = result.reshape(tall, columns, 2, LANES).transpose(0, 2, 1, 3)
     return spread.reshape(1, tall, 2, half)
 

time: 68.7 us -> 64 us (0.932)
  the two profiles are of different devices: /device:TPU:14 before, /device:TPU:1 now
where the time goes in v3:
time: 64 us; the launch traced here: 62.9 us
  Pallas kernels  62.9 us (98%)
    pallas_call x1, Pallas kernels, shards(): pl.pallas_call(functools.partial(kernel, gz, xy, chunks), out_shape=jax.S...  61.9 us

profile of v3, /device:TPU:1, one launch (start us, length us, event | category | flops | bytes accessed | tf_op | source)
XLA Modules:
  0.0 62.9 jit_solution(13907481409490003612)
XLA Ops:
  0.0 61.9 %shard_map.55.held_ref = f32[2048,128]{1,0:T(8,128)S(1)} custom-call(s32[64]{0:T(128)} %frequency_ref.1, f32[2,352,128]{2,1,0:T(8,128)} %constant.2.clone.seed_ref, bf16[64,32,128]{2,1,0:T(8,128)(2,1)} %fx_ref.1, bf16[64,32,128]{2,1,0:T(8,128)(2,1)} %fy_ref.1, bf16[64,32,128]{2,1,0:T(8,128)(2,1)} %fz_ref.1), custom_call_target="tpu_custom_call" | custom-call | tf_op jit(solution)/shard_map/pallas_call | solution.py:360
  62.0 1.0 %shard_map.56 = f32[2048,128]{1,0:T(8,128)} custom-call(f32[2048,128]{1,0:T(8,128)S(1)} %shard_map.55.held_ref), custom_call_target="tpu_custom_call" | custom-call | tf_op jit(solution)/shard_map/pallas_call | solution.py:402

commit v4 on v3

--- a/solution.py
+++ b/solution.py
@@ -15,6 +15,7 @@
 LANES = 128
 ROWS = 16
 STRIDE = 27
+GROUP = 8
 CODE_MAX = 32767.0
 TINY = 1e-30
 
@@ -63,8 +64,8 @@
 def kernel(
     gz, xy, chunks, frequency_ref, seed_ref, fx_ref, fy_ref, fz_ref, out_ref,
     fx, fy, fz, seeds, weights, page, edge_out, edge_in, code1, side1, got1, gotside1, gotedge,
-    table_hi, table_lo, planes, even, odd, code2, side2, got2, gotside2, factor, sums,
-    frequency, load_sem, edge_sem, send1, recv1, send2, recv2,
+    table_hi, table_lo, even, odd, code2, side2, got2, gotside2, factor, sums,
+    frequency, met_sem, load_sem, edge_sem, send1, recv1, send2, recv2,
 ):
     g = lax.axis_index("gz")
     r = lax.axis_index("xy")
@@ -90,7 +91,7 @@
 
     for i in range(1, xy):
         peer = lax.rem(r + i, xy)
-        pl.semaphore_signal(barrier, inc=1, device_id={"xy": peer}, device_id_type=MESH)
+        pl.semaphore_signal(barrier, inc=1, device_id={"gz": g - lax.rem(g, GROUP), "xy": peer}, device_id_type=MESH)
 
     loads[0].wait()
     for y in range(gz):
@@ -127,16 +128,13 @@
     def _(y):
         edge_out[y] = page[pl.ds(y, 1), :]
 
-    pl.semaphore_wait(barrier, gz + xy - 2)
-
-    edge_copy = pltpu.make_async_remote_copy(
-        src_ref=edge_out, dst_ref=edge_in, send_sem=edge_sem.at[0], recv_sem=edge_sem.at[1],
-        device_id={"xy": lax.rem(r + 1, xy)}, device_id_type=MESH,
-    )
-
-    @pl.when(r < xy - 1)
-    def _():
-        edge_copy.start()
+    first = lax.rem(g, GROUP) == 0
+    pl.semaphore_wait(barrier, gz - 1 + jnp.where(first, GROUP * (xy - 1), 0))
+
+    @pl.when(first)
+    def _():
+        for i in range(1, GROUP):
+            pl.semaphore_signal(met_sem, inc=1, device_id={"gz": g + i}, device_id_type=MESH)
 
     def exchange1(source, target, which, peer):
         return pltpu.make_async_remote_copy(
@@ -152,16 +150,6 @@
 
     got1[g] = code1[g]
     gotside1[g] = side1[g]
-
-    @pl.when(r > 0)
-    def _():
-        edge_copy.wait_recv()
-
-        @pl.loop(1, gz)
-        def _(i):
-            exchange1(edge_in, gotedge, 2, lax.rem(g + i * STRIDE, gz)).start()
-
-        gotedge[g] = edge_in[g]
 
     loads[4].wait()
     blocks = half // ROWS
@@ -204,6 +192,29 @@
             at = (p * columns + a) * LANES
             factor[:, at : at + LANES] = gain * own / (base + 4.0 * sine * sine)
 
+    @pl.when(jnp.logical_not(first))
+    def _():
+        pl.semaphore_wait(met_sem, 1)
+
+    edge_copy = pltpu.make_async_remote_copy(
+        src_ref=edge_out, dst_ref=edge_in, send_sem=edge_sem.at[0], recv_sem=edge_sem.at[1],
+        device_id={"xy": lax.rem(r + 1, xy)}, device_id_type=MESH,
+    )
+
+    @pl.when(r < xy - 1)
+    def _():
+        edge_copy.start()
+
+    @pl.when(r > 0)
+    def _():
+        edge_copy.wait_recv()
+
+        @pl.loop(1, gz)
+        def _(i):
+            exchange1(edge_in, gotedge, 2, lax.rem(g + i * STRIDE, gz)).start()
+
+        gotedge[g] = edge_in[g]
+
     def all_but_one(ref, sem):
         part = ref.at[pl.ds(0, ref.shape[0] - 1)]
         return pltpu.make_async_copy(part, part, sem)
@@ -227,23 +238,25 @@
     all_but_one(gotside1, recv1.at[1]).wait()
     all_but_one(got1, recv1.at[0]).wait()
 
-    @pl.loop(0, gz, unroll=8)
-    def _(k):
-        value = got1[k].astype(jnp.int32).astype(f32) * gotside1[k, 0:1, :].astype(f32)
-        below = gotside1[jnp.maximum(k - 1, 0), 1:2, :].astype(f32)
-        value = value - jnp.where((plane == 0) & (k > 0), below, 0.0)
-        value = value - jnp.where(lane == 0, pltpu.roll(edges, lax.rem(LANES - k, LANES), 1), 0.0)
-        high, low = split(value)
-        at = pl.ds(pl.multiple_of(k * depth, depth), depth)
-        planes[at, :LANES] = high
-        planes[at, LANES:] = low
+    first_row = lax.broadcasted_iota(jnp.int32, (8, LANES), 0) == 0
+
+    def decoded(k):
+        side = gotside1[k].astype(f32)
+        value = got1[k].astype(jnp.int32).astype(f32) * side[0:1]
+        value = value - jnp.where(lane == 0, pltpu.roll(edges, (LANES - k) % LANES, 1), 0.0)
+        if k == 0:
+            return value
+        below = gotside1[k - 1].astype(f32)[1:2]
+        return jnp.concatenate([value[:8] - jnp.where(first_row, below, 0.0), value[8:]], axis=0)
+
+    def plane_block(first):
+        return jnp.concatenate([decoded(first // depth + i) for i in range(turn // depth)], axis=0)
 
     for b in range(half // turn):
         here = slice(b * turn, (b + 1) * turn)
-        there = slice(nz - (b + 1) * turn, nz - b * turn)
-        lower = mixed(mirror, planes[there, :])
+        lower = mixed(mirror, jnp.concatenate(split(plane_block(nz - (b + 1) * turn)), axis=1))
         lower = lower[:, :LANES] + lower[:, LANES:]
-        upper = planes[here, :LANES].astype(f32) + planes[here, LANES:].astype(f32)
+        upper = plane_block(b * turn)
         even[here, :LANES], even[here, LANES:] = split(upper + lower)
         odd[here, :LANES], odd[here, LANES:] = split(upper - lower)
 
@@ -255,10 +268,13 @@
 
     chunk = half // chunks
     group = xy // chunks
+    wings = chunks // 2
 
     @pl.loop(0, chunks)
     def _(c):
-        at_chunk = lax.rem(r // group + chunks // 2 + c, chunks)
+        side = lax.rem(r // (xy // 2) + 1 + c, 2)
+        along = lax.rem(lax.rem(r // group, wings) + wings // 2 + c // 2, wings)
+        at_chunk = side * wings + along
         here = pl.ds(pl.multiple_of(at_chunk * chunk, chunk), chunk)
         parts = []
         for p, folded in enumerate((even, odd)):
@@ -298,7 +314,7 @@
             parts.append(got2[source].astype(jnp.int32).astype(f32) * gotside2[source])
         return jnp.concatenate(parts, axis=1)
 
-    start = jnp.where(2 * r < xy, steps // 2, 0)
+    start = jnp.where(4 * lax.rem(r, xy // 2) < xy, 1, steps - 1)
     for i in range(steps):
         b = lax.rem(start + i, steps)
         upper = line_block(b * pair)
@@ -378,7 +394,6 @@
             pltpu.VMEM((rows_y, 1, LANES), f32),
             pltpu.VMEM((2, half, half), bf16),
             pltpu.VMEM((2, half, half), bf16),
-            pltpu.VMEM((nz, 2 * LANES), bf16),
             pltpu.VMEM((half, 2 * LANES), bf16),
             pltpu.VMEM((half, 2 * LANES), bf16),
             pltpu.VMEM((xy, tall, LANES), i16),
@@ -388,6 +403,7 @@
             pltpu.VMEM((tall, nz), f32),
             pltpu.VMEM((tall, nz), f32),
             pltpu.SMEM((rows_y,), jnp.int32),
+            pltpu.SemaphoreType.REGULAR,
             pltpu.SemaphoreType.DMA((5,)),
             pltpu.SemaphoreType.DMA((2,)),
             pltpu.SemaphoreType.DMA((3,)),

time: 64 us -> 61.6 us (0.963); the launches traced: 62.9 us -> 61.4 us
  Pallas kernels: 62.9 us -> 61.4 us
    pallas_call x1, Pallas kernels: 61.9 us -> 60.4 us  [shards(): pl.pallas_call(functools.partial(kernel, gz, xy, chunks), out_shape=jax.S...]
where the time goes in v4:
time: 61.6 us; the launch traced here: 61.4 us
  Pallas kernels  61.4 us (100%)
    pallas_call x1, Pallas kernels, shards(): pl.pallas_call(functools.partial(kernel, gz, xy, chunks), out_shape=jax.S...  60.4 us

profile of v4, /device:TPU:1, one launch (start us, length us, event | category | flops | bytes accessed | tf_op | source)
XLA Modules:
  0.0 61.4 jit_solution(15130797115603928512)
XLA Ops:
  0.0 60.4 %shard_map.55.held_ref = f32[2048,128]{1,0:T(8,128)S(1)} custom-call(s32[64]{0:T(128)} %frequency_ref.1, f32[2,352,128]{2,1,0:T(8,128)} %constant.2.clone.seed_ref, bf16[64,32,128]{2,1,0:T(8,128)(2,1)} %fx_ref.1, bf16[64,32,128]{2,1,0:T(8,128)(2,1)} %fy_ref.1, bf16[64,32,128]{2,1,0:T(8,128)(2,1)} %fz_ref.1), custom_call_target="tpu_custom_call" | custom-call | tf_op jit(solution)/shard_map/pallas_call | solution.py:376
  60.5 1.0 %shard_map.56 = f32[2048,128]{1,0:T(8,128)} custom-call(f32[2048,128]{1,0:T(8,128)S(1)} %shard_map.55.held_ref), custom_call_target="tpu_custom_call" | custom-call | tf_op jit(solution)/shard_map/pallas_call | solution.py:418

commit v5 on v4

--- a/solution.py
+++ b/solution.py
@@ -15,7 +15,7 @@
 LANES = 128
 ROWS = 16
 STRIDE = 27
-GROUP = 8
+GROUP = 4
 CODE_MAX = 32767.0
 TINY = 1e-30
 
@@ -150,6 +150,19 @@
 
     got1[g] = code1[g]
     gotside1[g] = side1[g]
+
+    @pl.when(jnp.logical_not(first))
+    def _():
+        pl.semaphore_wait(met_sem, 1)
+
+    edge_copy = pltpu.make_async_remote_copy(
+        src_ref=edge_out, dst_ref=edge_in, send_sem=edge_sem.at[0], recv_sem=edge_sem.at[1],
+        device_id={"xy": lax.rem(r + 1, xy)}, device_id_type=MESH,
+    )
+
+    @pl.when(r < xy - 1)
+    def _():
+        edge_copy.start()
 
     loads[4].wait()
     blocks = half // ROWS
@@ -191,19 +204,6 @@
             own = jnp.where(kx == 0, math.sqrt(0.5), 1.0)
             at = (p * columns + a) * LANES
             factor[:, at : at + LANES] = gain * own / (base + 4.0 * sine * sine)
-
-    @pl.when(jnp.logical_not(first))
-    def _():
-        pl.semaphore_wait(met_sem, 1)
-
-    edge_copy = pltpu.make_async_remote_copy(
-        src_ref=edge_out, dst_ref=edge_in, send_sem=edge_sem.at[0], recv_sem=edge_sem.at[1],
-        device_id={"xy": lax.rem(r + 1, xy)}, device_id_type=MESH,
-    )
-
-    @pl.when(r < xy - 1)
-    def _():
-        edge_copy.start()
 
     @pl.when(r > 0)
     def _():

time: 61.6 us -> 61.4 us (level)
  no operation moved by 1% of the time
where the time goes in v5:
time: 61.4 us; the launch traced here: 61.3 us
  Pallas kernels  61.3 us (100%)
    pallas_call x1, Pallas kernels, shards(): pl.pallas_call(functools.partial(kernel, gz, xy, chunks), out_shape=jax.S...  60.3 us

profile of v5, /device:TPU:1, one launch (start us, length us, event | category | flops | bytes accessed | tf_op | source)
XLA Modules:
  0.0 61.3 jit_solution(5119500163809693514)
XLA Ops:
  0.0 60.3 %shard_map.55.held_ref = f32[2048,128]{1,0:T(8,128)S(1)} custom-call(s32[64]{0:T(128)} %frequency_ref.1, f32[2,352,128]{2,1,0:T(8,128)} %constant.2.clone.seed_ref, bf16[64,32,128]{2,1,0:T(8,128)(2,1)} %fx_ref.1, bf16[64,32,128]{2,1,0:T(8,128)(2,1)} %fy_ref.1, bf16[64,32,128]{2,1,0:T(8,128)(2,1)} %fz_ref.1), custom_call_target="tpu_custom_call" | custom-call | tf_op jit(solution)/shard_map/pallas_call | solution.py:376
  60.3 1.0 %shard_map.56 = f32[2048,128]{1,0:T(8,128)} custom-call(f32[2048,128]{1,0:T(8,128)S(1)} %shard_map.55.held_ref), custom_call_target="tpu_custom_call" | custom-call | tf_op jit(solution)/shard_map/pallas_call | solution.py:418
